TPU v7x, 32 devices: a whole 2x2x4 slice. The times are simulated.
32 devices in a mesh: groups: 2 (over y), section: 4 (over x, core), lat: 4 (over z).
Axes of the slice: x: 2, y: 2, z: 4, core: 2. Of those that a mesh axis runs over, the one named last changes fastest.
Arguments:
- member_slabs: float32 [8, 16, 64, 768], P(('groups', 'section'), 'lat'), parts along dimension 0, may hold values from -6 to 6
- member_codes: int32 [2, 8], P(None, 'groups'), parts along dimension 1, may hold values from 0 to 31
- member_table: float32 [32, 768], replicated, may hold values from -4 to 4
- land_sea: int32 [16, 64], P('lat'), may hold values 0 or 1
- land_embed: float32 [4, 768], P('section'), may hold values from -4 to 4
- attention_gain: float32 [4, 768], P('section'), may hold values from 0.25 to 1.75
- project_in: bfloat16 [4, 768, 2304], P('section'), may hold values from -0.21875 to 0.21875
- logit_scale: float32 [4, 12], P('section'), may hold values from 3 to 25
- position_kernel: float32 [4, 5, 3, 768], P('section'), may hold values from -1.5 to 1.5
- project_out: bfloat16 [4, 768, 768], P('section'), may hold values from -0.21875 to 0.21875
- feed_gain: float32 [4, 768], P('section'), may hold values from 0.25 to 1.75
- expand_weight: bfloat16 [4, 768, 2048], P('section'), may hold values from -0.21875 to 0.21875
- reduce_weight: bfloat16 [4, 2048, 768], P('section'), may hold values from -0.125 to 0.125
- window_offset: int32 [4], P('section'), may hold values from 1 to 31
Outputs:
- updated_slabs: float32 [8, 16, 64, 768], P(('groups', 'section'), 'lat'), parts along dimension 0
There are 2 independent parts, one for each index of `groups`. A program takes and returns all parts, laid end to end along the dimension named above; an argument that names none is the same for every part. Nothing has to cross between parts.
Inputs may be any that keep to these rules, and one draw needn't show every extreme that they name: member_codes[t, m] names the perturbation embedding of member m at tick t. `land_sea`: 1 marks land.
All inputs are finite; a program needn't handle non-finite values. No bound on the sum of `land_sea` on one device may be relied on, other than what follows from the above.
Results may differ from a plain program's by a relative error of at most 0.0085.
Values may be sent and summed in bfloat16 or wider, within the bound.
A program may use at most 128 MiB of HBM per device.

v0:
```python
import functools
import math

import jax
import jax.numpy as jnp
from jax import lax
from jax.experimental import pallas as pl
from jax.experimental.pallas import tpu as pltpu
from jax.sharding import PartitionSpec as P

WIN_LAT = 4
WIN_LON = 32
TICKS = 2
EPSILON = 1e-06

F32 = jnp.float32
BF16 = jnp.bfloat16
LANES = 128
COLS = 256
MESH = pl.DeviceIdType.MESH


def norm_scale(values, gain_row):
    mean_square = jnp.mean(values * values, axis=-1, keepdims=True)
    return values * lax.rsqrt(mean_square + EPSILON) * gain_row


def dot(left, right):
    return jnp.dot(left, right, preferred_element_type=F32)


def head_unit(values, head_width):
    groups = []
    for start in range(0, values.shape[1], LANES):
        part = values[:, start : start + LANES]
        lane = lax.broadcasted_iota(jnp.int32, part.shape, 1)
        square = part * part
        factor = None
        for low in range(0, LANES, head_width):
            inside = (lane >= low) & (lane < low + head_width)
            total = jnp.sum(jnp.where(inside, square, 0.0), axis=-1, keepdims=True)
            scale = lax.rsqrt(total + EPSILON)
            factor = scale if factor is None else jnp.where(inside, scale, factor)
        groups.append((part * factor).astype(BF16))
    return jnp.concatenate(groups, axis=1)


def split_index(index, length, count):
    whole = jnp.zeros_like(index)
    for step in range(1, count):
        whole = whole + (index >= step * length).astype(jnp.int32)
    return whole, index - whole * length


def kernel(
    sizes,
    codes,
    offsets,
    head_scale,
    slab,
    table,
    land,
    land_embed,
    attention_gain,
    feed_gain,
    position_kernel,
    in_hbm,
    out_hbm,
    up_hbm,
    down_hbm,
    result,
    w_in,
    w_out,
    w_up,
    w_down,
    stream,
    mixed,
    normed,
    halo,
    queries,
    keys,
    values,
    blended,
    normed_mix,
    hidden,
    window,
    land_column,
    ring_out,
    ring_in,
    weight_sem,
    halo_send,
    halo_recv,
    ring_send,
    ring_recv,
):
    section_count, band_count, lon_cells, head_width = sizes
    tokens, features = slab.shape
    band_rows = tokens // lon_cells
    half = tokens // 2
    per_group = LANES // head_width
    section = lax.axis_index("section")
    band = lax.axis_index("lat")
    following = lax.rem(section + 1, section_count)
    preceding = lax.rem(section + section_count - 1, section_count)
    has_low = band > 0
    has_high = band < band_count - 1
    shifted = lax.rem(section, 2)

    barrier = pltpu.get_barrier_semaphore()
    pl.semaphore_signal(barrier, inc=1, device_id={"section": following}, device_id_type=MESH)
    pl.semaphore_signal(barrier, inc=1, device_id={"section": preceding}, device_id_type=MESH)

    @pl.when(has_low)
    def _():
        pl.semaphore_signal(barrier, inc=1, device_id={"lat": band - 1}, device_id_type=MESH)

    @pl.when(has_high)
    def _():
        pl.semaphore_signal(barrier, inc=1, device_id={"lat": band + 1}, device_id_type=MESH)

    loads = [
        pltpu.make_async_copy(source, target, weight_sem.at[index])
        for index, (source, target) in enumerate(
            ((out_hbm, w_out), (up_hbm, w_up), (down_hbm, w_down))
        )
    ]
    in_loads = []
    for start in range(0, features, COLS):
        for base in range(0, 3 * features, features):
            columns = pl.ds(base + start, COLS)
            in_loads.append(
                pltpu.make_async_copy(
                    in_hbm.at[:, columns], w_in.at[:, columns], weight_sem.at[3 + len(in_loads)]
                )
            )
    for load in in_loads:
        load.start()

    square = (lon_cells, lon_cells)
    diagonal = lax.broadcasted_iota(jnp.int32, square, 0) == lax.broadcasted_iota(jnp.int32, square, 1)
    for row in range(band_rows):
        marks = jnp.broadcast_to(land[row : row + 1, :].astype(F32), square)
        land_column[row * lon_cells : (row + 1) * lon_cells, :] = jnp.sum(
            jnp.where(diagonal, marks, 0.0), axis=-1, keepdims=True
        )

    offset = offsets[0] * shifted
    key_starts = [half * (1 - shifted), half + half * shifted]
    for side in range(2):
        shape = (half, tokens)
        first_row = band * band_rows - band_rows // 2 + (
            (1 - shifted) * (band_rows // 2) if side == 0 else (1 + shifted) * (band_rows // 2)
        )
        _, query_lon = split_index(lax.broadcasted_iota(jnp.int32, shape, 0), lon_cells, band_rows)
        key_row, key_lon = split_index(lax.broadcasted_iota(jnp.int32, shape, 1), lon_cells, band_rows)
        tiles = []
        for lon in (query_lon, key_lon):
            moved = lon - offset
            moved = jnp.where(moved < 0, moved + lon_cells, moved)
            tiles.append(split_index(moved, WIN_LON, lon_cells // WIN_LON)[0])
        row = key_row + first_row
        inside = (tiles[0] == tiles[1]) & (row >= 0) & (row < band_rows * band_count)
        window[side] = jnp.where(inside, 1.0, 0.0)

    def project(source, target_rows, with_queries, loading):
        def step(index, carry):
            if loading:
                for load in in_loads[3 * index : 3 * index + 3]:
                    load.wait()
            start = index * COLS
            columns = pl.ds(start, COLS)
            rows = source[...]
            if with_queries:
                queries[:, columns] = head_unit(dot(rows, w_in[:, columns]), head_width)
            key = head_unit(
                dot(rows, w_in[:, pl.ds(features + start, COLS)]), head_width
            )
            value = dot(
                rows, w_in[:, pl.ds(2 * features + start, COLS)]
            ).astype(BF16)
            done = 0
            for first, count in target_rows:
                keys[first : first + count, columns] = key[done : done + count]
                values[first : first + count, columns] = value[done : done + count]
                done += count
            return carry

        for index in range(features // COLS):
            step(index, 0)

    def attend(index, carry):
        columns = pl.ds(index * LANES, LANES)
        lane = lax.broadcasted_iota(jnp.int32, (1, LANES), 1)
        own = [
            jnp.where((lane >= low) & (lane < low + head_width), 1.0, 0.0).astype(BF16)
            for low in range(0, LANES, head_width)
        ]
        taps = [
            [position_kernel[lat * 3 + lon, :, columns] for lon in range(3)]
            for lat in range(WIN_LAT + 1)
        ]
        for side in range(2):
            spots = []
            for row in range(side * band_rows // 2, (side + 1) * band_rows // 2):
                strips = [
                    values[(row + lat) * lon_cells : (row + lat + 1) * lon_cells, columns].astype(F32)
                    for lat in range(WIN_LAT + 1)
                ]
                parts = []
                for lon in range(3):
                    part = taps[0][lon] * strips[0]
                    for lat in range(1, WIN_LAT + 1):
                        part = part + taps[lat][lon] * strips[lat]
                    parts.append(part)
                spots.append(
                    parts[1]
                    + pltpu.roll(parts[0], 1, 0)
                    + pltpu.roll(parts[2], lon_cells - 1, 0)
                )
            total = jnp.concatenate(spots, axis=0)
            near = pl.ds(pl.multiple_of(key_starts[side], half), tokens)
            key = keys[near, columns]
            value = values[near, columns]
            query = queries[side * half : (side + 1) * half, columns]
            scores = lax.dot_general(
                jnp.concatenate([query * mark for mark in own], axis=0),
                key,
                (((1,), (1,)), ((), ())),
                preferred_element_type=F32,
            )
            weights = []
            for head in range(per_group):
                mine = scores[head * half : (head + 1) * half]
                raised = jnp.exp(mine * head_scale[index * per_group + head]) * window[side]
                inverse = 1.0 / jnp.sum(raised, axis=-1, keepdims=True)
                weights.append((raised * inverse).astype(BF16))
            found = dot(jnp.concatenate(weights, axis=0), value)
            attended = found[:half]
            for head in range(1, per_group):
                attended = jnp.where(
                    lane >= head * head_width, found[head * half : (head + 1) * half], attended
                )
            total = total + attended
            blended[side * half : (side + 1) * half, columns] = total.astype(BF16)
        return carry

    def expand(index, carry):
        columns = pl.ds(index * COLS, COLS)
        wide = dot(normed_mix[...], w_up[:, columns])
        hidden[:, columns] = (wide * 0.5 * (1.0 + lax.erf(wide * math.sqrt(0.5)))).astype(BF16)
        return carry

    def halo_copies(tick):
        up = pltpu.make_async_remote_copy(
            src_ref=normed.at[tick, pl.ds(half, half)],
            dst_ref=halo.at[tick, pl.ds(0, half)],
            send_sem=halo_send.at[tick, 0],
            recv_sem=halo_recv.at[tick, 0],
            device_id={"lat": jnp.minimum(band + 1, band_count - 1)},
            device_id_type=MESH,
        )
        down = pltpu.make_async_remote_copy(
            src_ref=normed.at[tick, pl.ds(0, half)],
            dst_ref=halo.at[tick, pl.ds(half, half)],
            send_sem=halo_send.at[tick, 1],
            recv_sem=halo_recv.at[tick, 1],
            device_id={"lat": jnp.maximum(band - 1, 0)},
            device_id_type=MESH,
        )
        return up, down

    def ring_copy(tick, part):
        columns = pl.ds(part * COLS, COLS)
        return pltpu.make_async_remote_copy(
            src_ref=ring_out.at[tick, :, columns],
            dst_ref=ring_in.at[tick, :, columns],
            send_sem=ring_send.at[tick, part],
            recv_sem=ring_recv.at[tick, part],
            device_id={"section": following},
            device_id_type=MESH,
        )

    parts = features // COLS
    for tick in range(TICKS):
        if tick:
            for part in range(parts):
                ring_copy(tick - 1, part).wait()
        member = lax.rem(section - tick + section_count * TICKS, section_count)
        code = codes[tick, member]
        table_row = lax.broadcasted_iota(jnp.int32, table.shape, 0)
        perturb = jnp.sum(jnp.where(table_row == code, table[...], 0.0), axis=0, keepdims=True)

        def enter(index, carry):
            rows = pl.ds(index * lon_cells, lon_cells)
            current = slab[rows, :] if tick == 0 else ring_in[tick - 1, rows, :].astype(F32)
            current = current + perturb + land_column[rows, :] * land_embed[...]
            stream[rows, :] = current
            normed[tick, rows, :] = norm_scale(current, attention_gain[...]).astype(BF16)
            return carry

        for index in range(band_rows):
            enter(index, 0)

        if tick == 0:
            ends = (band == 0).astype(jnp.int32) + (band == band_count - 1).astype(jnp.int32)
            pl.semaphore_wait(barrier, 4 - ends)

        up, down = halo_copies(tick)

        @pl.when(has_high)
        def _():
            up.start()

        @pl.when(has_low)
        def _():
            down.start()

        @pl.when(jnp.logical_not(has_low))
        def _():
            halo[tick, 0:half, :] = jnp.zeros((half, features), BF16)

        @pl.when(jnp.logical_not(has_high))
        def _():
            halo[tick, half:tokens, :] = jnp.zeros((half, features), BF16)

        if tick == 0:
            for load in loads:
                load.start()
        project(normed.at[tick], ((half, tokens),), True, tick == 0)

        @pl.when(has_high)
        def _():
            up.wait_send()
            down.wait_recv()

        @pl.when(has_low)
        def _():
            down.wait_send()
            up.wait_recv()

        project(halo.at[tick], ((0, half), (half + tokens, half)), False, False)
        for index in range(features // LANES):
            attend(index, 0)

        if tick == 0:
            loads[0].wait()
        for part in range(parts):
            columns = slice(part * COLS, (part + 1) * COLS)
            mixed[:, columns] = stream[:, columns] + dot(blended[...], w_out[:, columns])

        def middle(index, carry):
            rows = pl.ds(index * lon_cells, lon_cells)
            normed_mix[rows, :] = norm_scale(mixed[rows, :], feed_gain[...]).astype(BF16)
            return carry

        for index in range(band_rows):
            middle(index, 0)
        if tick == 0:
            loads[1].wait()
        for index in range(w_up.shape[1] // COLS):
            expand(index, 0)
        if tick == 0:
            loads[2].wait()
        for part in range(parts):
            columns = slice(part * COLS, (part + 1) * COLS)
            finished = mixed[:, columns] + dot(hidden[...], w_down[:, columns])
            if tick + 1 < TICKS:
                ring_out[tick, :, columns] = finished.astype(BF16)
                ring_copy(tick, part).start()
            else:
                result[:, columns] = finished


def solution(mesh):
    section_count = mesh.shape["section"]
    band_count = mesh.shape["lat"]

    def body(
        member_slabs,
        member_codes,
        member_table,
        land_sea,
        land_embed,
        attention_gain,
        project_in,
        logit_scale,
        position_kernel,
        project_out,
        feed_gain,
        expand_weight,
        reduce_weight,
        window_offset,
    ):
        _, band_rows, lon_cells, features = member_slabs.shape
        assert band_rows == WIN_LAT
        tokens = band_rows * lon_cells
        hidden_width = expand_weight.shape[2]
        head_width = features // logit_scale.shape[1]
        parts = features // COLS
        links = max(TICKS - 1, 1)
        smem = pl.BlockSpec(memory_space=pltpu.SMEM)
        vmem = pl.BlockSpec(memory_space=pltpu.VMEM)
        hbm = pl.BlockSpec(memory_space=pl.ANY)
        updated = pl.pallas_call(
            functools.partial(kernel, (section_count, band_count, lon_cells, head_width)),
            out_shape=jax.ShapeDtypeStruct((tokens, features), F32),
            in_specs=[smem] * 3 + [vmem] * 7 + [hbm] * 4,
            out_specs=vmem,
            scratch_shapes=[
                pltpu.VMEM((features, 3 * features), BF16),
                pltpu.VMEM((features, features), BF16),
                pltpu.VMEM((features, hidden_width), BF16),
                pltpu.VMEM((hidden_width, features), BF16),
                pltpu.VMEM((tokens, features), F32),
                pltpu.VMEM((tokens, features), F32),
                pltpu.VMEM((TICKS, tokens, features), BF16),
                pltpu.VMEM((TICKS, tokens, features), BF16),
                pltpu.VMEM((tokens, features), BF16),
                pltpu.VMEM((2 * tokens, features), BF16),
                pltpu.VMEM((2 * tokens, features), BF16),
                pltpu.VMEM((tokens, features), BF16),
                pltpu.VMEM((tokens, features), BF16),
                pltpu.VMEM((tokens, hidden_width), BF16),
                pltpu.VMEM((2, tokens // 2, tokens), F32),
                pltpu.VMEM((tokens, 1), F32),
                pltpu.VMEM((links, tokens, features), BF16),
                pltpu.VMEM((links, tokens, features), BF16),
                pltpu.SemaphoreType.DMA((3 + 3 * parts,)),
                pltpu.SemaphoreType.DMA((TICKS, 2)),
                pltpu.SemaphoreType.DMA((TICKS, 2)),
                pltpu.SemaphoreType.DMA((links, parts)),
                pltpu.SemaphoreType.DMA((links, parts)),
            ],
            compiler_params=pltpu.CompilerParams(
                collective_id=0, has_side_effects=True, vmem_limit_bytes=60 * 1024 * 1024
            ),
        )(
            member_codes,
            window_offset,
            logit_scale[0],
            member_slabs.reshape(tokens, features),
            member_table,
            land_sea,
            land_embed,
            attention_gain,
            feed_gain,
            position_kernel.reshape(-1, 1, features),
            project_in[0],
            project_out[0],
            expand_weight[0],
            reduce_weight[0],
        )
        return updated.reshape(member_slabs.shape)

    placed = (
        P(("groups", "section"), "lat", None, None),
        P(None, "groups"),
        P(),
        P("lat", None),
        P("section", None),
        P("section", None),
        P("section", None, None),
        P("section", None),
        P("section", None, None, None),
        P("section", None, None),
        P("section", None),
        P("section", None, None),
        P("section", None, None),
        P("section"),
    )
    return jax.shard_map(
        body,
        mesh=mesh,
        in_specs=placed,
        out_specs=P(("groups", "section"), "lat", None, None),
        check_vma=False,
    )
```

profile of v0, /device:TPU:0, one launch (start us, length us, event | category | flops | bytes accessed | tf_op | source)
XLA Modules:
  0.0 36.4 jit_solution(2870661297490310167)
XLA Ops:
  0.7 33.7 %shard_map.136 = f32[256,768]{1,0:T(8,128)} custom-call(s32[2,4]{1,0:T(2,128)} %codes.1, s32[1]{0:T(128)S(6)} %copy.16.offsets, f32[12]{0:T(128)} %bitcast.15, f32[256,768]{1,0:T(8,128)} %bitcast.13, f32[32,768]{1,0:T(8,128)} %table.1, s32[4,64]{1,0:T(4,128)} %land.1, f32[1,768]{1,0:T(1,128)} %land_embed.1, f32[1,768]{1,0:T(1,128)} %attention_gain.1, ...), custom_call_target="tpu_custom_call" | custom-call | tf_op jit(solution)/shard_map/pallas_call | solution.py:404
  34.3 2.1 %copy.17 = f32[1,4,64,768]{3,2,1,0:T(8,128)} copy(f32[1,4,64,768]{3,2,1,0:T(8,128)} %bitcast.9) | data formatting | bytes 1572864
where the time goes:
time: 36.6 us; the launch traced here: 36.4 us
  Pallas kernels  33.7 us (92%)
  local copies, waits for them, and re-layouts  2.09 us (6%)
  between operations  0.66 us (2%)
    pallas_call x1, Pallas kernels, body(): pl.pallas_call(functools.partial(kernel, (section_count, band_count, lon_...  33.7 us
    unnamed x1, local copies, waits for them, and re-layouts  2.09 us

commit v1 on v0

v1 whole, which is shorter than its diff:
```python
import contextlib
import functools
import math

import jax
import jax.numpy as jnp
from jax import lax
from jax.experimental import pallas as pl
from jax.experimental.pallas import tpu as pltpu
from jax.sharding import PartitionSpec as P

WIN_LAT = 4
WIN_LON = 32
TICKS = 2
EPSILON = 1e-06

F32 = jnp.float32
BF16 = jnp.bfloat16
LANES = 128
COLS = 256
ROWS = 32
AHEAD = 1
MESH = pl.DeviceIdType.MESH


def mark(name):
    return contextlib.nullcontext()


def norm_scale(values, gain_row):
    mean_square = jnp.mean(values * values, axis=-1, keepdims=True)
    return values * lax.rsqrt(mean_square + EPSILON) * gain_row


def dot(left, right):
    return jnp.dot(left, right, preferred_element_type=F32)


def head_unit(values, head_width):
    groups = []
    for start in range(0, values.shape[1], LANES):
        part = values[:, start : start + LANES]
        lane = lax.broadcasted_iota(jnp.int32, part.shape, 1)
        square = part * part
        factor = None
        for low in range(0, LANES, head_width):
            inside = (lane >= low) & (lane < low + head_width)
            total = jnp.sum(jnp.where(inside, square, 0.0), axis=-1, keepdims=True)
            scale = lax.rsqrt(total + EPSILON)
            factor = scale if factor is None else jnp.where(inside, scale, factor)
        groups.append((part * factor).astype(BF16))
    return jnp.concatenate(groups, axis=1)


def kernel(
    sizes,
    codes_hbm,
    offsets_hbm,
    scale_hbm,
    slab_hbm,
    table_hbm,
    land_hbm,
    embed_hbm,
    attention_gain_hbm,
    feed_gain_hbm,
    taps_hbm,
    in_hbm,
    out_hbm,
    up_hbm,
    down_hbm,
    result,
    codes,
    offsets,
    head_scale,
    slab,
    table,
    land,
    land_embed,
    attention_gain,
    feed_gain,
    position_kernel,
    w_in,
    w_out,
    w_up,
    w_down,
    stream,
    mixed,
    normed_here,
    normed,
    halo,
    queries,
    keys,
    values,
    attended,
    position,
    rolled,
    blended,
    normed_mix,
    hidden,
    order,
    land_column,
    ring_out,
    ring_in,
    load_sem,
    halo_send,
    halo_recv,
    ring_send,
    ring_recv,
):
    section_count, band_count, head_width = sizes
    pieces, band_rows, span, features = slab.shape
    lon_cells = pieces * span
    chunk = band_rows * span
    half = chunk // 2
    tokens = pieces * chunk
    per_group = LANES // head_width
    parts = features // COLS
    section = lax.axis_index("section")
    band = lax.axis_index("lat")
    following = lax.rem(section + 1, section_count)
    preceding = lax.rem(section + section_count - 1, section_count)
    has_low = band > 0
    has_high = band < band_count - 1
    shifted = lax.rem(section, 2)
    odd = shifted == 1
    even = shifted == 0

    barrier = pltpu.get_barrier_semaphore()
    pl.semaphore_signal(barrier, inc=1, device_id={"section": following}, device_id_type=MESH)
    pl.semaphore_signal(barrier, inc=1, device_id={"section": preceding}, device_id_type=MESH)

    @pl.when(has_low)
    def _():
        pl.semaphore_signal(barrier, inc=1, device_id={"lat": band - 1}, device_id_type=MESH)

    @pl.when(has_high)
    def _():
        pl.semaphore_signal(barrier, inc=1, device_id={"lat": band + 1}, device_id_type=MESH)

    pairs = [
        (slab_hbm.at[:, pl.ds(piece * span, span), :], slab.at[piece]) for piece in range(pieces)
    ]
    pairs += [
        (codes_hbm, codes),
        (offsets_hbm, offsets),
        (scale_hbm, head_scale),
        (table_hbm, table),
        (land_hbm, land),
        (embed_hbm, land_embed),
        (attention_gain_hbm, attention_gain),
        (feed_gain_hbm, feed_gain),
        (taps_hbm, position_kernel),
    ]
    small = len(pairs)
    for start in range(0, features, COLS):
        for base in range(0, 3 * features, features):
            columns = pl.ds(base + start, COLS)
            pairs.append((in_hbm.at[:, columns], w_in.at[:, columns]))
    wide = len(pairs)
    pairs += [(out_hbm, w_out), (up_hbm, w_up), (down_hbm, w_down)]
    loads = [
        pltpu.make_async_copy(source, target, load_sem.at[index])
        for index, (source, target) in enumerate(pairs)
    ]
    for load in loads:
        load.start()

    @pl.when(jnp.logical_not(has_low))
    def _():
        halo[:, 0] = jnp.zeros(halo.shape[:1] + halo.shape[2:], BF16)

    @pl.when(jnp.logical_not(has_high))
    def _():
        halo[:, 1] = jnp.zeros(halo.shape[:1] + halo.shape[2:], BF16)

    with mark("small"):
        for load in loads[:small]:
            load.wait()

    offset = offsets[0, 0]
    square = (lon_cells, lon_cells)
    diagonal = lax.broadcasted_iota(jnp.int32, square, 0) == lax.broadcasted_iota(jnp.int32, square, 1)
    for row in range(band_rows):
        marks = jnp.broadcast_to(land[row : row + 1, :].astype(F32), square)
        column = jnp.sum(jnp.where(diagonal, marks, 0.0), axis=-1, keepdims=True)
        for piece in range(pieces):
            first = piece * chunk + row * span
            land_column[first : first + span, :] = column[piece * span : (piece + 1) * span]

    def fill_order():
        for way, turn in enumerate((offset, lon_cells - offset)):
            for piece in range(pieces):
                for row in range(band_rows):
                    lon = lax.broadcasted_iota(jnp.int32, (span, tokens), 0) + piece * span + turn
                    lon = jnp.where(lon >= lon_cells, lon - lon_cells, lon)
                    target = lon + row * span
                    for step in range(1, pieces):
                        target = target + jnp.where(lon >= step * span, chunk - span, 0)
                    source = lax.broadcasted_iota(jnp.int32, (span, tokens), 1)
                    first = piece * chunk + row * span
                    order[way, first : first + span, :] = jnp.where(target == source, 1.0, 0.0).astype(BF16)

    lane = lax.broadcasted_iota(jnp.int32, (1, LANES), 1)
    own = [
        jnp.where((lane >= low) & (lane < low + head_width), 1.0, 0.0).astype(BF16)
        for low in range(0, LANES, head_width)
    ]
    key_lane = lax.broadcasted_iota(jnp.int32, (1, chunk), 1)
    keeps = [
        jnp.where((key_lane >= half) | has_low, 1.0, 0.0),
        jnp.where((key_lane < half) | has_high, 1.0, 0.0),
    ]

    def halo_up(tick, piece):
        return pltpu.make_async_remote_copy(
            src_ref=normed.at[tick, piece, pl.ds(half, half)],
            dst_ref=halo.at[tick, 0, piece],
            send_sem=halo_send.at[tick, piece, 0],
            recv_sem=halo_recv.at[tick, piece, 0],
            device_id={"lat": jnp.minimum(band + 1, band_count - 1)},
            device_id_type=MESH,
        )

    def halo_down(tick, piece):
        return pltpu.make_async_remote_copy(
            src_ref=normed.at[tick, piece, pl.ds(0, half)],
            dst_ref=halo.at[tick, 1, piece],
            send_sem=halo_send.at[tick, piece, 1],
            recv_sem=halo_recv.at[tick, piece, 1],
            device_id={"lat": jnp.maximum(band - 1, 0)},
            device_id_type=MESH,
        )

    def start_halo(tick, which):
        @pl.when(has_high)
        def _():
            for piece in which:
                halo_up(tick, piece).start()

        @pl.when(has_low)
        def _():
            for piece in which:
                halo_down(tick, piece).start()

    def wait_halo(tick):
        @pl.when(has_high)
        def _():
            for piece in range(pieces):
                halo_down(tick, piece).wait_recv()

        @pl.when(has_low)
        def _():
            for piece in range(pieces):
                halo_up(tick, piece).wait_recv()

    def drain_halo(tick):
        @pl.when(has_high)
        def _():
            for piece in range(pieces):
                halo_up(tick, piece).wait_send()

        @pl.when(has_low)
        def _():
            for piece in range(pieces):
                halo_down(tick, piece).wait_send()

    def ring_copy(tick, piece):
        return pltpu.make_async_remote_copy(
            src_ref=ring_out.at[tick, piece],
            dst_ref=ring_in.at[tick, piece],
            send_sem=ring_send.at[tick, piece],
            recv_sem=ring_recv.at[tick, piece],
            device_id={"section": following},
            device_id_type=MESH,
        )

    def wait_barrier():
        ends = (band == 0).astype(jnp.int32) + (band == band_count - 1).astype(jnp.int32)
        pl.semaphore_wait(barrier, 4 - ends)

    def enter(tick, piece, perturb, target):
        for row in range(band_rows):
            first = row * span
            rows = slice(piece * chunk + first, piece * chunk + first + span)
            if tick == 0:
                current = slab[piece, row]
            else:
                current = ring_in[tick - 1, piece, first : first + span, :].astype(F32)
            current = current + perturb + land_column[rows, :] * land_embed[...]
            stream[rows, :] = current
            target[piece, first : first + span, :] = norm_scale(current, attention_gain[...]).astype(BF16)

    def roll_rows(way, source, store):
        for part in range(parts):
            columns = slice(part * COLS, (part + 1) * COLS)
            for piece in range(pieces):
                moved = dot(order[way, piece * chunk : (piece + 1) * chunk, :], source(columns))
                store(piece, columns, moved.astype(BF16))

    def project_own(tick, piece):
        rows = normed[tick, piece]
        for part in range(parts):
            start = part * COLS
            columns = slice(start, start + COLS)
            queries[piece, :, columns] = head_unit(dot(rows, w_in[:, columns]), head_width)
            keys[piece, half : half + chunk, columns] = head_unit(
                dot(rows, w_in[:, features + start : features + start + COLS]), head_width
            )
            values[piece, half : half + chunk, columns] = dot(
                rows, w_in[:, 2 * features + start : 2 * features + start + COLS]
            ).astype(BF16)

    def project_halo(tick, with_keys):
        for part in range(parts):
            start = part * COLS
            columns = slice(start, start + COLS)
            for side in range(2):
                rows = halo[tick, side].reshape(pieces * half, features)
                first = side * (half + chunk)
                value = dot(rows, w_in[:, 2 * features + start : 2 * features + start + COLS]).astype(BF16)
                if with_keys:
                    key = head_unit(
                        dot(rows, w_in[:, features + start : features + start + COLS]), head_width
                    )
                for piece in range(pieces):
                    mine = slice(piece * half, (piece + 1) * half)
                    values[piece, first : first + half, columns] = value[mine]
                    if with_keys:
                        keys[piece, first : first + half, columns] = key[mine]

    def soften(scores, group, head, keep):
        factor = head_scale[group * per_group + head] * math.log2(math.e)
        raised = jnp.exp2(scores * factor)
        if keep is not None:
            raised = raised * keep
        return (raised * (1.0 / jnp.sum(raised, axis=-1, keepdims=True))).astype(BF16)

    def score_even(piece, group):
        columns = slice(group * LANES, (group + 1) * LANES)
        key = keys[piece, half : half + chunk, columns]
        return lax.dot_general(
            queries[piece, :, columns],
            jnp.concatenate([key * mark_row for mark_row in own], axis=0),
            (((1,), (1,)), ((), ())),
            preferred_element_type=F32,
        )

    def mix_even(piece, group, scores):
        columns = slice(group * LANES, (group + 1) * LANES)
        value = values[piece, half : half + chunk, columns]
        weights = [
            soften(scores[:, head * chunk : (head + 1) * chunk], group, head, None)
            for head in range(per_group)
        ]
        attended[piece, :, columns] = dot(
            jnp.concatenate(weights, axis=1),
            jnp.concatenate([value * mark_row for mark_row in own], axis=0),
        )

    def score_odd(piece, group):
        columns = slice(group * LANES, (group + 1) * LANES)
        query = queries[piece, :, columns]
        return lax.dot_general(
            jnp.concatenate([query * mark_row for mark_row in own], axis=0),
            keys[piece, :, columns],
            (((1,), (1,)), ((), ())),
            preferred_element_type=F32,
        )

    def mix_odd(piece, group, scores):
        columns = slice(group * LANES, (group + 1) * LANES)
        for side in range(2):
            value = values[piece, side * chunk : (side + 1) * chunk, columns]
            weights = []
            for head in range(per_group):
                first = head * chunk + side * half
                mine = scores[first : first + half, side * chunk : (side + 1) * chunk]
                weights.append(soften(mine, group, head, keeps[side]))
            attended[piece, side * half : (side + 1) * half, columns] = dot(
                jnp.concatenate(weights, axis=1),
                jnp.concatenate([value * mark_row for mark_row in own], axis=0),
            )

    def attend(some_pieces, score, mix):
        waiting = []
        for piece in some_pieces:
            for group in range(features // LANES):
                waiting.append((piece, group, score(piece, group)))
                if len(waiting) > AHEAD:
                    mix(*waiting.pop(0))
        for unit in waiting:
            mix(*unit)

    def spread(group, inner, store):
        columns = slice(group * LANES, (group + 1) * LANES)
        reach = WIN_LAT // 2
        for row in range(band_rows):
            steps = [
                step
                for step in range(WIN_LAT + 1)
                if (0 <= row + step - reach < band_rows) == inner
            ]
            sums = [None] * 3
            for step in steps:
                strip = jnp.concatenate(
                    [
                        values[piece, (row + step) * span : (row + step + 1) * span, columns]
                        for piece in range(pieces)
                    ],
                    axis=0,
                ).astype(F32)
                for lon in range(3):
                    term = position_kernel[step * 3 + lon, :, columns] * strip
                    sums[lon] = term if sums[lon] is None else sums[lon] + term
            total = sums[1] + pltpu.roll(sums[0], 1, 0) + pltpu.roll(sums[2], lon_cells - 1, 0)
            store(row, columns, total)

    def spread_own():
        for group in range(features // LANES):

            def store(row, columns, total):
                for piece in range(pieces):
                    position[piece, row * span : (row + 1) * span, columns] = total[
                        piece * span : (piece + 1) * span
                    ]

            spread(group, True, store)

    def blend(target):
        for group in range(features // LANES):

            def store(row, columns, total):
                for piece in range(pieces):
                    rows = slice(row * span, (row + 1) * span)
                    target[piece, rows, columns] = (
                        total[piece * span : (piece + 1) * span]
                        + position[piece, rows, columns]
                        + attended[piece, rows, columns]
                    ).astype(BF16)

            spread(group, False, store)

    for tick in range(TICKS):
        member = lax.rem(section - tick + section_count * TICKS, section_count)
        code = codes[tick, member]
        table_row = lax.broadcasted_iota(jnp.int32, table.shape, 0)
        perturb = jnp.sum(jnp.where(table_row == code, table[...], 0.0), axis=0, keepdims=True)
        everything = range(pieces)

        @pl.when(even)
        def _():
            for piece in everything:
                if tick:
                    with mark(f"e{tick}ring{piece}"):
                        ring_copy(tick - 1, piece).wait_recv()
                with mark(f"e{tick}enter{piece}"):
                    enter(tick, piece, perturb, normed.at[tick])
                if tick:
                    start_halo(tick, [piece])
                elif piece == 0:
                    with mark("e0load"):
                        for load in loads[small:wide]:
                            load.wait()
                with mark(f"e{tick}own{piece}"):
                    project_own(tick, piece)
                    attend([piece], score_even, mix_even)
            if tick == 0:
                with mark("e0barrier"):
                    wait_barrier()
                start_halo(tick, everything)
            with mark(f"e{tick}spread"):
                spread_own()
            with mark(f"e{tick}halowait"):
                wait_halo(tick)
            with mark(f"e{tick}after"):
                project_halo(tick, False)
                blend(blended)

        @pl.when(odd)
        def _():
            for piece in everything:
                if tick:
                    with mark(f"o{tick}ring{piece}"):
                        ring_copy(tick - 1, piece).wait_recv()
                with mark(f"o{tick}enter{piece}"):
                    enter(tick, piece, perturb, normed_here)
            with mark(f"o{tick}roll"):
                if tick == 0:
                    fill_order()

                def take(columns):
                    return normed_here[:, :, columns].reshape(tokens, COLS)

                def give(piece, columns, moved):
                    normed[tick, piece, :, columns] = moved

                roll_rows(0, take, give)
            if tick == 0:
                with mark("o0barrier"):
                    wait_barrier()
            start_halo(tick, everything)
            if tick == 0:
                with mark("o0load"):
                    for load in loads[small:wide]:
                        load.wait()
            with mark(f"o{tick}own"):
                for piece in everything:
                    project_own(tick, piece)
                spread_own()
            with mark(f"o{tick}halowait"):
                wait_halo(tick)
            with mark(f"o{tick}after"):
                project_halo(tick, True)
                attend(everything, score_odd, mix_odd)
                blend(rolled)

                def take_back(columns):
                    return rolled[:, :, columns].reshape(tokens, COLS)

                def give_back(piece, columns, moved):
                    blended[piece, :, columns] = moved

                roll_rows(1, take_back, give_back)

        drain_halo(tick)
        if tick == 0:
            with mark("load2"):
                for load in loads[wide:]:
                    load.wait()
        for piece in everything:
            with mark(f"t{tick}mlp{piece}"):
                rows = slice(piece * chunk, (piece + 1) * chunk)
                for part in range(parts):
                    columns = slice(part * COLS, (part + 1) * COLS)
                    mixed[rows, columns] = stream[rows, columns] + dot(blended[piece], w_out[:, columns])
                for first in range(piece * chunk, (piece + 1) * chunk, ROWS):
                    block = slice(first, first + ROWS)
                    normed_mix[block, :] = norm_scale(mixed[block, :], feed_gain[...]).astype(BF16)
                for start in range(0, w_up.shape[1], COLS):
                    columns = slice(start, start + COLS)
                    raw = dot(normed_mix[rows, :], w_up[:, columns])
                    hidden[rows, columns] = (raw * 0.5 * (1.0 + lax.erf(raw * math.sqrt(0.5)))).astype(BF16)
                middle = w_down.shape[0] // 2
                for part in range(parts):
                    columns = slice(part * COLS, (part + 1) * COLS)
                    finished = (
                        mixed[rows, columns]
                        + dot(hidden[rows, :middle], w_down[:middle, columns])
                        + dot(hidden[rows, middle:], w_down[middle:, columns])
                    )
                    if tick + 1 < TICKS:
                        ring_out[tick, piece, :, columns] = finished.astype(BF16)
                    else:
                        for row in range(band_rows):
                            result[row * lon_cells + piece * span : row * lon_cells + (piece + 1) * span, columns] = (
                                finished[row * span : (row + 1) * span]
                            )
            if tick + 1 < TICKS:
                ring_copy(tick, piece).start()

    for tick in range(TICKS - 1):
        for piece in range(pieces):
            ring_copy(tick, piece).wait_send()


def solution(mesh):
    section_count = mesh.shape["section"]
    band_count = mesh.shape["lat"]

    def body(
        member_slabs,
        member_codes,
        member_table,
        land_sea,
        land_embed,
        attention_gain,
        project_in,
        logit_scale,
        position_kernel,
        project_out,
        feed_gain,
        expand_weight,
        reduce_weight,
        window_offset,
    ):
        _, band_rows, lon_cells, features = member_slabs.shape
        assert band_rows == WIN_LAT
        tokens = band_rows * lon_cells
        pieces = lon_cells // WIN_LON
        chunk = tokens // pieces
        half = chunk // 2
        hidden_width = expand_weight.shape[2]
        heads = logit_scale.shape[1]
        head_width = features // heads
        links = max(TICKS - 1, 1)
        taps = position_kernel.reshape(-1, 1, features)
        operands = (
            member_codes,
            window_offset.reshape(1, 1),
            logit_scale[0],
            member_slabs[0],
            member_table,
            land_sea,
            land_embed,
            attention_gain,
            feed_gain,
            taps,
            project_in[0],
            project_out[0],
            expand_weight[0],
            reduce_weight[0],
        )
        updated = pl.pallas_call(
            functools.partial(kernel, (section_count, band_count, head_width)),
            out_shape=pltpu.VMEM((tokens, features), F32),
            in_specs=[pl.BlockSpec(memory_space=pltpu.HBM)] * len(operands),
            out_specs=pl.BlockSpec(memory_space=pltpu.VMEM),
            scratch_shapes=[
                pltpu.SMEM(member_codes.shape, jnp.int32),
                pltpu.SMEM((1, 1), jnp.int32),
                pltpu.SMEM((heads,), F32),
                pltpu.VMEM((pieces, band_rows, WIN_LON, features), F32),
                pltpu.VMEM(member_table.shape, F32),
                pltpu.VMEM(land_sea.shape, jnp.int32),
                pltpu.VMEM(land_embed.shape, F32),
                pltpu.VMEM(attention_gain.shape, F32),
                pltpu.VMEM(feed_gain.shape, F32),
                pltpu.VMEM(taps.shape, F32),
                pltpu.VMEM((features, 3 * features), BF16),
                pltpu.VMEM((features, features), BF16),
                pltpu.VMEM((features, hidden_width), BF16),
                pltpu.VMEM((hidden_width, features), BF16),
                pltpu.VMEM((tokens, features), F32),
                pltpu.VMEM((tokens, features), F32),
                pltpu.VMEM((pieces, chunk, features), BF16),
                pltpu.VMEM((TICKS, pieces, chunk, features), BF16),
                pltpu.VMEM((TICKS, 2, pieces, half, features), BF16),
                pltpu.VMEM((pieces, chunk, features), BF16),
                pltpu.VMEM((pieces, 2 * chunk, features), BF16),
                pltpu.VMEM((pieces, 2 * chunk, features), BF16),
                pltpu.VMEM((pieces, chunk, features), F32),
                pltpu.VMEM((pieces, chunk, features), F32),
                pltpu.VMEM((pieces, chunk, features), BF16),
                pltpu.VMEM((pieces, chunk, features), BF16),
                pltpu.VMEM((tokens, features), BF16),
                pltpu.VMEM((tokens, hidden_width), BF16),
                pltpu.VMEM((2, tokens, tokens), BF16),
                pltpu.VMEM((tokens, 1), F32),
                pltpu.VMEM((links, pieces, chunk, features), BF16),
                pltpu.VMEM((links, pieces, chunk, features), BF16),
                pltpu.SemaphoreType.DMA((pieces + 12 + 3 * (features // COLS),)),
                pltpu.SemaphoreType.DMA((TICKS, pieces, 2)),
                pltpu.SemaphoreType.DMA((TICKS, pieces, 2)),
                pltpu.SemaphoreType.DMA((links, pieces)),
                pltpu.SemaphoreType.DMA((links, pieces)),
            ],
            compiler_params=pltpu.CompilerParams(
                collective_id=0, has_side_effects=True, vmem_limit_bytes=40 * 1024 * 1024
            ),
        )(
            *[
                operand if operand.size == 1 else pltpu.with_memory_space_constraint(operand, pltpu.HBM)
                for operand in operands
            ]
        )
        return updated.reshape(member_slabs.shape)

    placed = (
        P(("groups", "section"), "lat", None, None),
        P(None, "groups"),
        P(),
        P("lat", None),
        P("section", None),
        P("section", None),
        P("section", None, None),
        P("section", None),
        P("section", None, None, None),
        P("section", None, None),
        P("section", None),
        P("section", None, None),
        P("section", None, None),
        P("section"),
    )
    return jax.shard_map(
        body,
        mesh=mesh,
        in_specs=placed,
        out_specs=P(("groups", "section"), "lat", None, None),
        check_vma=False,
    )
```

time: 36.6 us -> 31.1 us (0.85)
  the two profiles are of different devices: /device:TPU:0 before, /device:TPU:1 now
where the time goes in v1:
time: 31.1 us; the launch traced here: 30.9 us
  Pallas kernels  29.4 us (95%)
  local copies, waits for them, and re-layouts  0.88 us (3%)
  between operations  0.66 us (2%)
    pallas_call x1, Pallas kernels, body(): pl.pallas_call(functools.partial(kernel, (section_count, band_count, head...  29.4 us
    unnamed x1, local copies, waits for them, and re-layouts  0.88 us

profile of v1, /device:TPU:1, one launch (start us, length us, event | category | flops | bytes accessed | tf_op | source)
XLA Modules:
  0.0 30.9 jit_solution(14734029201540913277)
XLA Ops:
  0.7 29.4 %shard_map.136 = f32[256,768]{1,0:T(8,128)S(1)} custom-call(s32[2,4]{1,0:T(2,128)} %codes_hbm.1, s32[1,1]{1,0:T(1,128)} %bitcast.9.offsets_hbm, f32[12]{0:T(128)} %bitcast.17, f32[4,64,768]{2,1,0:T(8,128)} %bitcast.15, f32[32,768]{1,0:T(8,128)} %table_hbm.1, s32[4,64]{1,0:T(4,128)} %land_hbm.1, f32[1,768]{1,0:T(1,128)} %embed_hbm.1, ...), custom_call_target="tpu_custom_call" | custom-call | tf_op jit(solution)/shard_map/pallas_call | solution.py:613
  30.0 0.9 %copy.16 = f32[1,4,64,768]{3,2,1,0:T(8,128)} copy(f32[1,4,64,768]{3,2,1,0:T(8,128)S(1)} %bitcast.10) | data formatting | bytes 1572864

commit v2 on v1

--- a/solution.py
+++ b/solution.py
@@ -19,7 +19,7 @@
 LANES = 128
 COLS = 256
 ROWS = 32
-AHEAD = 1
+AHEAD = 2
 MESH = pl.DeviceIdType.MESH
 
 
@@ -97,6 +97,7 @@
     blended,
     normed_mix,
     hidden,
+    partial,
     order,
     land_column,
     ring_out,
@@ -152,10 +153,7 @@
         (taps_hbm, position_kernel),
     ]
     small = len(pairs)
-    for start in range(0, features, COLS):
-        for base in range(0, 3 * features, features):
-            columns = pl.ds(base + start, COLS)
-            pairs.append((in_hbm.at[:, columns], w_in.at[:, columns]))
+    pairs.append((in_hbm, w_in))
     wide = len(pairs)
     pairs += [(out_hbm, w_out), (up_hbm, w_up), (down_hbm, w_down)]
     loads = [
@@ -167,27 +165,28 @@
 
     @pl.when(jnp.logical_not(has_low))
     def _():
-        halo[:, 0] = jnp.zeros(halo.shape[:1] + halo.shape[2:], BF16)
+        halo[:, :, 0] = jnp.zeros(halo.shape[:2] + halo.shape[3:], BF16)
 
     @pl.when(jnp.logical_not(has_high))
     def _():
-        halo[:, 1] = jnp.zeros(halo.shape[:1] + halo.shape[2:], BF16)
-
-    with mark("small"):
-        for load in loads[:small]:
-            load.wait()
-
-    offset = offsets[0, 0]
-    square = (lon_cells, lon_cells)
-    diagonal = lax.broadcasted_iota(jnp.int32, square, 0) == lax.broadcasted_iota(jnp.int32, square, 1)
-    for row in range(band_rows):
-        marks = jnp.broadcast_to(land[row : row + 1, :].astype(F32), square)
-        column = jnp.sum(jnp.where(diagonal, marks, 0.0), axis=-1, keepdims=True)
-        for piece in range(pieces):
-            first = piece * chunk + row * span
-            land_column[first : first + span, :] = column[piece * span : (piece + 1) * span]
+        halo[:, :, 1] = jnp.zeros(halo.shape[:2] + halo.shape[3:], BF16)
+
+    def settle():
+        with mark("small"):
+            for load in loads[:small]:
+                load.wait()
+
+        square = (lon_cells, lon_cells)
+        diagonal = lax.broadcasted_iota(jnp.int32, square, 0) == lax.broadcasted_iota(jnp.int32, square, 1)
+        for row in range(band_rows):
+            marks = jnp.broadcast_to(land[row : row + 1, :].astype(F32), square)
+            column = jnp.sum(jnp.where(diagonal, marks, 0.0), axis=-1, keepdims=True)
+            for piece in range(pieces):
+                first = piece * chunk + row * span
+                land_column[first : first + span, :] = column[piece * span : (piece + 1) * span]
 
     def fill_order():
+        offset = offsets[0, 0]
         for way, turn in enumerate((offset, lon_cells - offset)):
             for piece in range(pieces):
                 for row in range(band_rows):
@@ -214,7 +213,7 @@
     def halo_up(tick, piece):
         return pltpu.make_async_remote_copy(
             src_ref=normed.at[tick, piece, pl.ds(half, half)],
-            dst_ref=halo.at[tick, 0, piece],
+            dst_ref=halo.at[tick, piece, 0],
             send_sem=halo_send.at[tick, piece, 0],
             recv_sem=halo_recv.at[tick, piece, 0],
             device_id={"lat": jnp.minimum(band + 1, band_count - 1)},
@@ -224,7 +223,7 @@
     def halo_down(tick, piece):
         return pltpu.make_async_remote_copy(
             src_ref=normed.at[tick, piece, pl.ds(0, half)],
-            dst_ref=halo.at[tick, 1, piece],
+            dst_ref=halo.at[tick, piece, 1],
             send_sem=halo_send.at[tick, piece, 1],
             recv_sem=halo_recv.at[tick, piece, 1],
             device_id={"lat": jnp.maximum(band - 1, 0)},
@@ -242,16 +241,14 @@
             for piece in which:
                 halo_down(tick, piece).start()
 
-    def wait_halo(tick):
+    def wait_halo(tick, piece):
         @pl.when(has_high)
         def _():
-            for piece in range(pieces):
-                halo_down(tick, piece).wait_recv()
+            halo_down(tick, piece).wait_recv()
 
         @pl.when(has_low)
         def _():
-            for piece in range(pieces):
-                halo_up(tick, piece).wait_recv()
+            halo_up(tick, piece).wait_recv()
 
     def drain_halo(tick):
         @pl.when(has_high)
@@ -273,6 +270,11 @@
             device_id={"section": following},
             device_id_type=MESH,
         )
+
+    def wait_weights():
+        with mark("weights"):
+            for load in loads[wide:]:
+                load.wait()
 
     def wait_barrier():
         ends = (band == 0).astype(jnp.int32) + (band == band_count - 1).astype(jnp.int32)
@@ -291,9 +293,9 @@
             target[piece, first : first + span, :] = norm_scale(current, attention_gain[...]).astype(BF16)
 
     def roll_rows(way, source, store):
-        for part in range(parts):
-            columns = slice(part * COLS, (part + 1) * COLS)
-            for piece in range(pieces):
+        for piece in range(pieces):
+            for part in range(parts):
+                columns = slice(part * COLS, (part + 1) * COLS)
                 moved = dot(order[way, piece * chunk : (piece + 1) * chunk, :], source(columns))
                 store(piece, columns, moved.astype(BF16))
 
@@ -310,23 +312,22 @@
                 rows, w_in[:, 2 * features + start : 2 * features + start + COLS]
             ).astype(BF16)
 
-    def project_halo(tick, with_keys):
+    def project_halo(tick, piece, with_keys):
+        rows = halo[tick, piece].reshape(2 * half, features)
         for part in range(parts):
             start = part * COLS
             columns = slice(start, start + COLS)
+            value = dot(rows, w_in[:, 2 * features + start : 2 * features + start + COLS]).astype(BF16)
+            if with_keys:
+                key = head_unit(
+                    dot(rows, w_in[:, features + start : features + start + COLS]), head_width
+                )
             for side in range(2):
-                rows = halo[tick, side].reshape(pieces * half, features)
+                mine = slice(side * half, (side + 1) * half)
                 first = side * (half + chunk)
-                value = dot(rows, w_in[:, 2 * features + start : 2 * features + start + COLS]).astype(BF16)
+                values[piece, first : first + half, columns] = value[mine]
                 if with_keys:
-                    key = head_unit(
-                        dot(rows, w_in[:, features + start : features + start + COLS]), head_width
-                    )
-                for piece in range(pieces):
-                    mine = slice(piece * half, (piece + 1) * half)
-                    values[piece, first : first + half, columns] = value[mine]
-                    if with_keys:
-                        keys[piece, first : first + half, columns] = key[mine]
+                    keys[piece, first : first + half, columns] = key[mine]
 
     def soften(scores, group, head, keep):
         factor = head_scale[group * per_group + head] * math.log2(math.e)
@@ -440,44 +441,80 @@
 
             spread(group, False, store)
 
-    for tick in range(TICKS):
+    def leave(some_pieces):
+        for piece in some_pieces:
+            rows = slice(piece * chunk, (piece + 1) * chunk)
+            for part in range(parts):
+                columns = slice(part * COLS, (part + 1) * COLS)
+                mixed[rows, columns] = stream[rows, columns] + dot(blended[piece], w_out[:, columns])
+        for piece in some_pieces:
+            for first in range(piece * chunk, (piece + 1) * chunk, ROWS):
+                block = slice(first, first + ROWS)
+                normed_mix[block, :] = norm_scale(mixed[block, :], feed_gain[...]).astype(BF16)
+
+    def expand(piece):
+        rows = slice(piece * chunk, (piece + 1) * chunk)
+        for start in range(0, w_up.shape[1], COLS):
+            columns = slice(start, start + COLS)
+            raw = dot(normed_mix[rows, :], w_up[:, columns])
+            hidden[rows, columns] = (raw * 0.5 * (1.0 + lax.erf(raw * math.sqrt(0.5)))).astype(BF16)
+
+    def finish(tick, at_once):
+        with mark(f"t{tick}out"):
+            leave(range(pieces) if at_once else [0])
+        for piece in range(pieces):
+            with mark(f"t{tick}mlp{piece}"):
+                expand(piece)
+                if not at_once and piece + 1 < pieces:
+                    leave([piece + 1])
+                contract(tick, piece)
+            if tick + 1 < TICKS:
+                ring_copy(tick, piece).start()
+
+    def contract(tick, piece):
+        rows = slice(piece * chunk, (piece + 1) * chunk)
+        middle = w_down.shape[0] // 2
+        for part in range(parts):
+            columns = slice(part * COLS, (part + 1) * COLS)
+            if part + 1 == parts and parts % 2:
+                partial[...] = dot(hidden[rows, :middle], w_down[:middle, columns])
+                finished = (
+                    mixed[rows, columns] + dot(hidden[rows, middle:], w_down[middle:, columns])
+                ) + partial[...]
+            else:
+                finished = mixed[rows, columns] + dot(hidden[rows, :], w_down[:, columns])
+            if tick + 1 < TICKS:
+                ring_out[tick, piece, :, columns] = finished.astype(BF16)
+            else:
+                for row in range(band_rows):
+                    first = row * lon_cells + piece * span
+                    result[first : first + span, columns] = finished[row * span : (row + 1) * span]
+
+    everything = range(pieces)
+
+    def embedding(tick):
         member = lax.rem(section - tick + section_count * TICKS, section_count)
         code = codes[tick, member]
         table_row = lax.broadcasted_iota(jnp.int32, table.shape, 0)
-        perturb = jnp.sum(jnp.where(table_row == code, table[...], 0.0), axis=0, keepdims=True)
-        everything = range(pieces)
-
-        @pl.when(even)
-        def _():
-            for piece in everything:
-                if tick:
-                    with mark(f"e{tick}ring{piece}"):
-                        ring_copy(tick - 1, piece).wait_recv()
-                with mark(f"e{tick}enter{piece}"):
-                    enter(tick, piece, perturb, normed.at[tick])
-                if tick:
-                    start_halo(tick, [piece])
-                elif piece == 0:
-                    with mark("e0load"):
-                        for load in loads[small:wide]:
-                            load.wait()
-                with mark(f"e{tick}own{piece}"):
-                    project_own(tick, piece)
-                    attend([piece], score_even, mix_even)
-            if tick == 0:
-                with mark("e0barrier"):
-                    wait_barrier()
-                start_halo(tick, everything)
-            with mark(f"e{tick}spread"):
-                spread_own()
-            with mark(f"e{tick}halowait"):
-                wait_halo(tick)
-            with mark(f"e{tick}after"):
-                project_halo(tick, False)
-                blend(blended)
-
-        @pl.when(odd)
-        def _():
+        return jnp.sum(jnp.where(table_row == code, table[...], 0.0), axis=0, keepdims=True)
+
+    def wait_inputs():
+        with mark("inload"):
+            for load in loads[small:wide]:
+                load.wait()
+
+    def drain():
+        for tick in range(TICKS):
+            drain_halo(tick)
+            if tick + 1 < TICKS:
+                for piece in everything:
+                    ring_copy(tick, piece).wait_send()
+
+    @pl.when(odd)
+    def _():
+        settle()
+        for tick in range(TICKS):
+            perturb = embedding(tick)
             for piece in everything:
                 if tick:
                     with mark(f"o{tick}ring{piece}"):
@@ -498,20 +535,25 @@
             if tick == 0:
                 with mark("o0barrier"):
                     wait_barrier()
-            start_halo(tick, everything)
+            start_halo(tick, [0])
             if tick == 0:
-                with mark("o0load"):
-                    for load in loads[small:wide]:
-                        load.wait()
-            with mark(f"o{tick}own"):
-                for piece in everything:
+                wait_inputs()
+            for piece in everything:
+                with mark(f"o{tick}own{piece}"):
                     project_own(tick, piece)
+                if piece + 1 < pieces:
+                    start_halo(tick, [piece + 1])
+            with mark(f"o{tick}spread"):
                 spread_own()
-            with mark(f"o{tick}halowait"):
-                wait_halo(tick)
-            with mark(f"o{tick}after"):
-                project_halo(tick, True)
-                attend(everything, score_odd, mix_odd)
+            if tick == 0:
+                wait_weights()
+            for piece in everything:
+                with mark(f"o{tick}halowait{piece}"):
+                    wait_halo(tick, piece)
+                with mark(f"o{tick}after{piece}"):
+                    project_halo(tick, piece, True)
+                    attend([piece], score_odd, mix_odd)
+            with mark(f"o{tick}blend"):
                 blend(rolled)
 
                 def take_back(columns):
@@ -521,46 +563,46 @@
                     blended[piece, :, columns] = moved
 
                 roll_rows(1, take_back, give_back)
-
-        drain_halo(tick)
-        if tick == 0:
-            with mark("load2"):
-                for load in loads[wide:]:
-                    load.wait()
-        for piece in everything:
-            with mark(f"t{tick}mlp{piece}"):
-                rows = slice(piece * chunk, (piece + 1) * chunk)
-                for part in range(parts):
-                    columns = slice(part * COLS, (part + 1) * COLS)
-                    mixed[rows, columns] = stream[rows, columns] + dot(blended[piece], w_out[:, columns])
-                for first in range(piece * chunk, (piece + 1) * chunk, ROWS):
-                    block = slice(first, first + ROWS)
-                    normed_mix[block, :] = norm_scale(mixed[block, :], feed_gain[...]).astype(BF16)
-                for start in range(0, w_up.shape[1], COLS):
-                    columns = slice(start, start + COLS)
-                    raw = dot(normed_mix[rows, :], w_up[:, columns])
-                    hidden[rows, columns] = (raw * 0.5 * (1.0 + lax.erf(raw * math.sqrt(0.5)))).astype(BF16)
-                middle = w_down.shape[0] // 2
-                for part in range(parts):
-                    columns = slice(part * COLS, (part + 1) * COLS)
-                    finished = (
-                        mixed[rows, columns]
-                        + dot(hidden[rows, :middle], w_down[:middle, columns])
-                        + dot(hidden[rows, middle:], w_down[middle:, columns])
-                    )
-                    if tick + 1 < TICKS:
-                        ring_out[tick, piece, :, columns] = finished.astype(BF16)
-                    else:
-                        for row in range(band_rows):
-                            result[row * lon_cells + piece * span : row * lon_cells + (piece + 1) * span, columns] = (
-                                finished[row * span : (row + 1) * span]
-                            )
-            if tick + 1 < TICKS:
-                ring_copy(tick, piece).start()
-
-    for tick in range(TICKS - 1):
-        for piece in range(pieces):
-            ring_copy(tick, piece).wait_send()
+            finish(tick, tick + 1 == TICKS)
+        drain()
+
+    @pl.when(even)
+    def _():
+        settle()
+        for tick in range(TICKS):
+            perturb = embedding(tick)
+            for piece in everything:
+                if tick:
+                    with mark(f"e{tick}ring{piece}"):
+                        ring_copy(tick - 1, piece).wait_recv()
+                with mark(f"e{tick}enter{piece}"):
+                    enter(tick, piece, perturb, normed.at[tick])
+                if tick and piece == pieces - 1:
+                    start_halo(tick, [piece])
+                if tick == 0 and piece == 0:
+                    wait_inputs()
+                with mark(f"e{tick}own{piece}"):
+                    project_own(tick, piece)
+                if tick == 0 and piece == 0:
+                    with mark("e0barrier"):
+                        wait_barrier()
+                if tick == 0 or piece < pieces - 1:
+                    start_halo(tick, [piece])
+                with mark(f"e{tick}own{piece}"):
+                    attend([piece], score_even, mix_even)
+            with mark(f"e{tick}spread"):
+                spread_own()
+            if tick == 0:
+                wait_weights()
+            for piece in everything:
+                with mark(f"e{tick}halowait{piece}"):
+                    wait_halo(tick, piece)
+                with mark(f"e{tick}after{piece}"):
+                    project_halo(tick, piece, False)
+                    if piece == pieces - 1:
+                        blend(blended)
+            finish(tick, True)
+        drain()
 
 
 def solution(mesh):
@@ -634,7 +676,7 @@
                 pltpu.VMEM((tokens, features), F32),
                 pltpu.VMEM((pieces, chunk, features), BF16),
                 pltpu.VMEM((TICKS, pieces, chunk, features), BF16),
-                pltpu.VMEM((TICKS, 2, pieces, half, features), BF16),
+                pltpu.VMEM((TICKS, pieces, 2, half, features), BF16),
                 pltpu.VMEM((pieces, chunk, features), BF16),
                 pltpu.VMEM((pieces, 2 * chunk, features), BF16),
                 pltpu.VMEM((pieces, 2 * chunk, features), BF16),
@@ -644,11 +686,12 @@
                 pltpu.VMEM((pieces, chunk, features), BF16),
                 pltpu.VMEM((tokens, features), BF16),
                 pltpu.VMEM((tokens, hidden_width), BF16),
+                pltpu.VMEM((chunk, COLS), F32),
                 pltpu.VMEM((2, tokens, tokens), BF16),
                 pltpu.VMEM((tokens, 1), F32),
                 pltpu.VMEM((links, pieces, chunk, features), BF16),
                 pltpu.VMEM((links, pieces, chunk, features), BF16),
-                pltpu.SemaphoreType.DMA((pieces + 12 + 3 * (features // COLS),)),
+                pltpu.SemaphoreType.DMA((pieces + 13,)),
                 pltpu.SemaphoreType.DMA((TICKS, pieces, 2)),
                 pltpu.SemaphoreType.DMA((TICKS, pieces, 2)),
                 pltpu.SemaphoreType.DMA((links, pieces)),

time: 31.1 us -> 27.2 us (0.87)
  the two profiles are of different devices: /device:TPU:1 before, /device:TPU:0 now
where the time goes in v2:
time: 27.2 us; the launch traced here: 27.1 us
  Pallas kernels  25.5 us (94%)
  local copies, waits for them, and re-layouts  0.88 us (3%)
  between operations  0.66 us (2%)
    pallas_call x1, Pallas kernels, body(): pl.pallas_call(functools.partial(kernel, (section_count, band_count, head...  25.5 us
    unnamed x1, local copies, waits for them, and re-layouts  0.88 us

profile of v2, /device:TPU:0, one launch (start us, length us, event | category | flops | bytes accessed | tf_op | source)
XLA Modules:
  0.0 27.1 jit_solution(6284369498134830939)
XLA Ops:
  0.7 25.5 %shard_map.136 = f32[256,768]{1,0:T(8,128)S(1)} custom-call(s32[2,4]{1,0:T(2,128)} %codes_hbm.1, s32[1,1]{1,0:T(1,128)} %bitcast.9.offsets_hbm, f32[12]{0:T(128)} %bitcast.17, f32[4,64,768]{2,1,0:T(8,128)} %bitcast.15, f32[32,768]{1,0:T(8,128)} %table_hbm.1, s32[4,64]{1,0:T(4,128)} %land_hbm.1, f32[1,768]{1,0:T(1,128)} %embed_hbm.1, ...), custom_call_target="tpu_custom_call" | custom-call | tf_op jit(solution)/shard_map/pallas_call | solution.py:655
  26.2 0.9 %copy.16 = f32[1,4,64,768]{3,2,1,0:T(8,128)} copy(f32[1,4,64,768]{3,2,1,0:T(8,128)S(1)} %bitcast.10) | data formatting | bytes 1572864

commit v3 on v2

--- a/solution.py
+++ b/solution.py
@@ -103,9 +103,7 @@
     ring_out,
     ring_in,
     load_sem,
-    halo_send,
     halo_recv,
-    ring_send,
     ring_recv,
 ):
     section_count, band_count, head_width = sizes
@@ -153,6 +151,7 @@
         (taps_hbm, position_kernel),
     ]
     small = len(pairs)
+    assert small >= TICKS * pieces * 2 + (TICKS - 1) * (pieces + 1)
     pairs.append((in_hbm, w_in))
     wide = len(pairs)
     pairs += [(out_hbm, w_out), (up_hbm, w_up), (down_hbm, w_down)]
@@ -171,9 +170,13 @@
     def _():
         halo[:, :, 1] = jnp.zeros(halo.shape[:2] + halo.shape[3:], BF16)
 
-    def settle():
+    def settle(with_order):
+        for load in loads[pieces : pieces + 2]:
+            load.wait()
+        if with_order:
+            fill_order()
         with mark("small"):
-            for load in loads[:small]:
+            for load in loads[pieces + 2 : small] + loads[:pieces]:
                 load.wait()
 
         square = (lon_cells, lon_cells)
@@ -214,7 +217,7 @@
         return pltpu.make_async_remote_copy(
             src_ref=normed.at[tick, piece, pl.ds(half, half)],
             dst_ref=halo.at[tick, piece, 0],
-            send_sem=halo_send.at[tick, piece, 0],
+            send_sem=load_sem.at[(tick * pieces + piece) * 2 + 0],
             recv_sem=halo_recv.at[tick, piece, 0],
             device_id={"lat": jnp.minimum(band + 1, band_count - 1)},
             device_id_type=MESH,
@@ -224,7 +227,7 @@
         return pltpu.make_async_remote_copy(
             src_ref=normed.at[tick, piece, pl.ds(0, half)],
             dst_ref=halo.at[tick, piece, 1],
-            send_sem=halo_send.at[tick, piece, 1],
+            send_sem=load_sem.at[(tick * pieces + piece) * 2 + 1],
             recv_sem=halo_recv.at[tick, piece, 1],
             device_id={"lat": jnp.maximum(band - 1, 0)},
             device_id_type=MESH,
@@ -261,15 +264,25 @@
             for piece in range(pieces):
                 halo_down(tick, piece).wait_send()
 
-    def ring_copy(tick, piece):
+    def ring_copy(tick, piece, part, wide):
+        columns = pl.ds(part * COLS, wide * COLS)
         return pltpu.make_async_remote_copy(
-            src_ref=ring_out.at[tick, piece],
-            dst_ref=ring_in.at[tick, piece],
-            send_sem=ring_send.at[tick, piece],
-            recv_sem=ring_recv.at[tick, piece],
+            src_ref=ring_out.at[tick, piece, :, columns],
+            dst_ref=ring_in.at[tick, piece, :, columns],
+            send_sem=load_sem.at[TICKS * pieces * 2 + tick * (pieces + 1) + piece + (part > 0) * pieces],
+            recv_sem=ring_recv.at[tick, piece + (part > 0) * pieces],
             device_id={"section": following},
             device_id_type=MESH,
         )
+
+    def ring_cuts(from_odd, piece):
+        if from_odd and piece == 0:
+            return [(0, parts - 1), (parts - 1, 1)]
+        return [(0, parts)]
+
+    def wait_ring(tick, piece, from_odd):
+        for cut in ring_cuts(from_odd, piece):
+            ring_copy(tick, piece, *cut).wait_recv()
 
     def wait_weights():
         with mark("weights"):
@@ -459,25 +472,26 @@
             raw = dot(normed_mix[rows, :], w_up[:, columns])
             hidden[rows, columns] = (raw * 0.5 * (1.0 + lax.erf(raw * math.sqrt(0.5)))).astype(BF16)
 
-    def finish(tick, at_once):
+    def finish(tick, from_odd):
+        last = tick + 1 == TICKS
+        staged = from_odd and not last
         with mark(f"t{tick}out"):
-            leave(range(pieces) if at_once else [0])
+            leave([0] if staged else range(pieces))
         for piece in range(pieces):
             with mark(f"t{tick}mlp{piece}"):
                 expand(piece)
-                if not at_once and piece + 1 < pieces:
+                if staged and piece + 1 < pieces:
                     leave([piece + 1])
-                contract(tick, piece)
-            if tick + 1 < TICKS:
-                ring_copy(tick, piece).start()
-
-    def contract(tick, piece):
+                contract(tick, piece, ring_cuts(from_odd, piece))
+
+    def contract(tick, piece, cuts):
         rows = slice(piece * chunk, (piece + 1) * chunk)
         middle = w_down.shape[0] // 2
+        if parts % 2:
+            partial[...] = dot(hidden[rows, :middle], w_down[:middle, (parts - 1) * COLS :])
         for part in range(parts):
             columns = slice(part * COLS, (part + 1) * COLS)
             if part + 1 == parts and parts % 2:
-                partial[...] = dot(hidden[rows, :middle], w_down[:middle, columns])
                 finished = (
                     mixed[rows, columns] + dot(hidden[rows, middle:], w_down[middle:, columns])
                 ) + partial[...]
@@ -485,6 +499,9 @@
                 finished = mixed[rows, columns] + dot(hidden[rows, :], w_down[:, columns])
             if tick + 1 < TICKS:
                 ring_out[tick, piece, :, columns] = finished.astype(BF16)
+                for cut in cuts:
+                    if part + 1 == sum(cut):
+                        ring_copy(tick, piece, *cut).start()
             else:
                 for row in range(band_rows):
                     first = row * lon_cells + piece * span
@@ -503,28 +520,26 @@
             for load in loads[small:wide]:
                 load.wait()
 
-    def drain():
+    def drain(from_odd):
         for tick in range(TICKS):
             drain_halo(tick)
             if tick + 1 < TICKS:
                 for piece in everything:
-                    ring_copy(tick, piece).wait_send()
+                    for cut in ring_cuts(from_odd, piece):
+                        ring_copy(tick, piece, *cut).wait_send()
 
     @pl.when(odd)
     def _():
-        settle()
+        settle(True)
         for tick in range(TICKS):
             perturb = embedding(tick)
             for piece in everything:
                 if tick:
                     with mark(f"o{tick}ring{piece}"):
-                        ring_copy(tick - 1, piece).wait_recv()
+                        wait_ring(tick - 1, piece, False)
                 with mark(f"o{tick}enter{piece}"):
                     enter(tick, piece, perturb, normed_here)
             with mark(f"o{tick}roll"):
-                if tick == 0:
-                    fill_order()
-
                 def take(columns):
                     return normed_here[:, :, columns].reshape(tokens, COLS)
 
@@ -563,21 +578,21 @@
                     blended[piece, :, columns] = moved
 
                 roll_rows(1, take_back, give_back)
-            finish(tick, tick + 1 == TICKS)
-        drain()
+            finish(tick, True)
+        drain(True)
 
     @pl.when(even)
     def _():
-        settle()
+        settle(False)
         for tick in range(TICKS):
             perturb = embedding(tick)
             for piece in everything:
                 if tick:
                     with mark(f"e{tick}ring{piece}"):
-                        ring_copy(tick - 1, piece).wait_recv()
+                        wait_ring(tick - 1, piece, True)
                 with mark(f"e{tick}enter{piece}"):
                     enter(tick, piece, perturb, normed.at[tick])
-                if tick and piece == pieces - 1:
+                if tick:
                     start_halo(tick, [piece])
                 if tick == 0 and piece == 0:
                     wait_inputs()
@@ -586,7 +601,7 @@
                 if tick == 0 and piece == 0:
                     with mark("e0barrier"):
                         wait_barrier()
-                if tick == 0 or piece < pieces - 1:
+                if tick == 0:
                     start_halo(tick, [piece])
                 with mark(f"e{tick}own{piece}"):
                     attend([piece], score_even, mix_even)
@@ -601,12 +616,13 @@
                     project_halo(tick, piece, False)
                     if piece == pieces - 1:
                         blend(blended)
-            finish(tick, True)
-        drain()
+            finish(tick, False)
+        drain(False)
 
 
 def solution(mesh):
     section_count = mesh.shape["section"]
+    assert section_count % 2 == 0
     band_count = mesh.shape["lat"]
 
     def body(
@@ -693,9 +709,7 @@
                 pltpu.VMEM((links, pieces, chunk, features), BF16),
                 pltpu.SemaphoreType.DMA((pieces + 13,)),
                 pltpu.SemaphoreType.DMA((TICKS, pieces, 2)),
-                pltpu.SemaphoreType.DMA((TICKS, pieces, 2)),
-                pltpu.SemaphoreType.DMA((links, pieces)),
-                pltpu.SemaphoreType.DMA((links, pieces)),
+                pltpu.SemaphoreType.DMA((links, pieces + 1)),
             ],
             compiler_params=pltpu.CompilerParams(
                 collective_id=0, has_side_effects=True, vmem_limit_bytes=40 * 1024 * 1024

time: 27.2 us -> 27 us (level)
  no operation moved by 1% of the time
where the time goes in v3:
time: 27 us; the launch traced here: 26.8 us
  Pallas kernels  25.3 us (94%)
  local copies, waits for them, and re-layouts  0.88 us (3%)
  between operations  0.66 us (2%)
    pallas_call x1, Pallas kernels, body(): pl.pallas_call(functools.partial(kernel, (section_count, band_count, head...  25.3 us
    unnamed x1, local copies, waits for them, and re-layouts  0.88 us

profile of v3, /device:TPU:0, one launch (start us, length us, event | category | flops | bytes accessed | tf_op | source)
XLA Modules:
  0.0 26.8 jit_solution(6855944956931448008)
XLA Ops:
  0.7 25.3 %shard_map.136 = f32[256,768]{1,0:T(8,128)S(1)} custom-call(s32[2,4]{1,0:T(2,128)} %codes_hbm.1, s32[1,1]{1,0:T(1,128)} %bitcast.9.offsets_hbm, f32[12]{0:T(128)} %bitcast.17, f32[4,64,768]{2,1,0:T(8,128)} %bitcast.15, f32[32,768]{1,0:T(8,128)} %table_hbm.1, s32[4,64]{1,0:T(4,128)} %land_hbm.1, f32[1,768]{1,0:T(1,128)} %embed_hbm.1, ...), custom_call_target="tpu_custom_call" | custom-call | tf_op jit(solution)/shard_map/pallas_call | solution.py:671
  26.0 0.9 %copy.16 = f32[1,4,64,768]{3,2,1,0:T(8,128)} copy(f32[1,4,64,768]{3,2,1,0:T(8,128)S(1)} %bitcast.10) | data formatting | bytes 1572864

commit v4 on v3

--- a/solution.py
+++ b/solution.py
@@ -305,12 +305,13 @@
             stream[rows, :] = current
             target[piece, first : first + span, :] = norm_scale(current, attention_gain[...]).astype(BF16)
 
-    def roll_rows(way, source, store):
+    def roll_rows(way, source, store, then):
         for piece in range(pieces):
             for part in range(parts):
                 columns = slice(part * COLS, (part + 1) * COLS)
                 moved = dot(order[way, piece * chunk : (piece + 1) * chunk, :], source(columns))
                 store(piece, columns, moved.astype(BF16))
+            then(piece)
 
     def project_own(tick, piece):
         rows = normed[tick, piece]
@@ -422,10 +423,12 @@
                         for piece in range(pieces)
                     ],
                     axis=0,
-                ).astype(F32)
+                )
+                strip = strip.astype(F32) if inner else strip
                 for lon in range(3):
-                    term = position_kernel[step * 3 + lon, :, columns] * strip
+                    term = position_kernel[step * 3 + lon, :, columns].astype(strip.dtype) * strip
                     sums[lon] = term if sums[lon] is None else sums[lon] + term
+            sums = [part.astype(F32) for part in sums]
             total = sums[1] + pltpu.roll(sums[0], 1, 0) + pltpu.roll(sums[2], lon_cells - 1, 0)
             store(row, columns, total)
 
@@ -546,11 +549,13 @@
                 def give(piece, columns, moved):
                     normed[tick, piece, :, columns] = moved
 
-                roll_rows(0, take, give)
-            if tick == 0:
-                with mark("o0barrier"):
-                    wait_barrier()
-            start_halo(tick, [0])
+                def send(piece):
+                    if piece == 0:
+                        if tick == 0:
+                            wait_barrier()
+                        start_halo(tick, [piece])
+
+                roll_rows(0, take, give, send)
             if tick == 0:
                 wait_inputs()
             for piece in everything:
@@ -577,7 +582,7 @@
                 def give_back(piece, columns, moved):
                     blended[piece, :, columns] = moved
 
-                roll_rows(1, take_back, give_back)
+                roll_rows(1, take_back, give_back, lambda piece: None)
             finish(tick, True)
         drain(True)
 

time: 27 us -> 26.9 us (level)
  no operation moved by 1% of the time
where the time goes in v4:
time: 26.9 us; the launch traced here: 26.8 us
  Pallas kernels  25.2 us (94%)
  local copies, waits for them, and re-layouts  0.88 us (3%)
  between operations  0.66 us (2%)
    pallas_call x1, Pallas kernels, body(): pl.pallas_call(functools.partial(kernel, (section_count, band_count, head...  25.2 us
    unnamed x1, local copies, waits for them, and re-layouts  0.88 us

profile of v4, /device:TPU:0, one launch (start us, length us, event | category | flops | bytes accessed | tf_op | source)
XLA Modules:
  0.0 26.8 jit_solution(10138916018064128708)
XLA Ops:
  0.7 25.2 %shard_map.136 = f32[256,768]{1,0:T(8,128)S(1)} custom-call(s32[2,4]{1,0:T(2,128)} %codes_hbm.1, s32[1,1]{1,0:T(1,128)} %bitcast.9.offsets_hbm, f32[12]{0:T(128)} %bitcast.17, f32[4,64,768]{2,1,0:T(8,128)} %bitcast.15, f32[32,768]{1,0:T(8,128)} %table_hbm.1, s32[4,64]{1,0:T(4,128)} %land_hbm.1, f32[1,768]{1,0:T(1,128)} %embed_hbm.1, ...), custom_call_target="tpu_custom_call" | custom-call | tf_op jit(solution)/shard_map/pallas_call | solution.py:676
  25.9 0.9 %copy.16 = f32[1,4,64,768]{3,2,1,0:T(8,128)} copy(f32[1,4,64,768]{3,2,1,0:T(8,128)S(1)} %bitcast.10) | data formatting | bytes 1572864
